TPU v7x, 32 devices: a whole 2x2x4 slice. The times are simulated.
32 devices in a mesh: grp: 4 (over z), head: 8 (over y, x, core).
Axes of the slice: x: 2, y: 2, z: 4, core: 2. Of those that a mesh axis runs over, the one named last changes fastest.
Arguments:
- inputs: bfloat16 [4, 64, 4096], P(None, 'grp', 'head'), parts along dimension 1, may hold values from -6 to 6
- gains: float32 [2, 4096], replicated, may hold values from 0.5 to 1.5
- decays: float32 [2, 32], P(None, 'head'), may hold values from 0.7 to 0.999
- w_qkv: bfloat16 [2, 4096, 3, 32, 128], P(None, None, None, 'head'), may hold values from -0.09375 to 0.09375
- w_out: bfloat16 [2, 32, 128, 4096], P(None, 'head'), may hold values from -0.125 to 0.125
- s_state: float32 [2, 64, 32, 128, 128], P(None, 'grp', 'head'), parts along dimension 1, may hold values from -0.5 to 0.5
- r_state: float32 [2, 64, 32, 128, 128], P(None, 'grp', 'head'), parts along dimension 1, as said below
Outputs:
- stream_out: float32 [4, 64, 4096], P(None, 'grp', 'head'), parts along dimension 1
- s_final: float32 [2, 64, 32, 128, 128], P(None, 'grp', 'head'), parts along dimension 1
- r_final: float32 [2, 64, 32, 128, 128], P(None, 'grp', 'head'), parts along dimension 1
There are 4 independent parts, one for each index of `grp`. A program takes and returns all parts, laid end to end along the dimension named above; an argument that names none is the same for every part. Nothing has to cross between parts.
Inputs may be any that keep to these rules, and one draw needn't show every extreme that they name: `r_state`: each matrix is symmetric positive definite with eigenvalues of 0.5 or more and of order one.
All inputs are finite; a program needn't handle non-finite values.
Results may differ from a plain program's by a relative error of at most 0.02.
Values may be sent and summed in bfloat16 or wider, within the bound.
A program may use at most 192 MiB of HBM per device.

v0:
```python
import functools

import jax
import jax.numpy as jnp
from jax import lax
from jax.experimental import pallas as pl
from jax.experimental.pallas import tpu as pltpu
from jax.sharding import PartitionSpec as P

EPSILON = 1e-05
RING = 4
CHUNK = 256
F32 = jnp.float32
BF16 = jnp.bfloat16
MESH = pl.DeviceIdType.MESH


def front_kernel(
    n, tokens, batch, heads, layers,
    x_ref, gains_ref, dec_ref, w_hbm, wo_hbm, s_hbm, r_hbm,
    y_ref, left_ref, right_ref,
    raw, wide, rep, wo, sv, rv, xg, lhs, acc, part, recv, cur, kq, pz, os, oo,
    raw_sem, in_sem, send_sem, recv_sem, own_sem,
):
    me = lax.axis_index("head")
    rows = tokens * batch
    hd = kq.shape[-1]
    width = lhs.shape[1]
    shard = x_ref.shape[1]
    mixed = 3 * heads
    chunks = width // CHUNK
    span = CHUNK * mixed

    def raw_copy(layer, c, slot):
        return pltpu.make_async_copy(
            w_hbm.at[layer, pl.ds(pl.multiple_of(c * span, span), span)],
            raw.at[slot],
            raw_sem.at[slot],
        )

    def state_copies(layer):
        return (
            pltpu.make_async_copy(r_hbm.at[layer], rv.at[layer], in_sem.at[0, layer]),
            pltpu.make_async_copy(s_hbm.at[layer], sv.at[layer], in_sem.at[1, layer]),
            pltpu.make_async_copy(wo_hbm.at[layer], wo.at[layer], in_sem.at[2, layer]),
        )

    def fill(layer):
        for c in range(min(RING, chunks)):
            raw_copy(layer, c, c).start()

    def repack(layer):
        def body(c, carry):
            slot = lax.rem(c, RING)
            raw_copy(layer, c, slot).wait()
            wide[...] = raw[slot].astype(F32)

            @pl.when(c + RING < chunks)
            def _():
                raw_copy(layer, c + RING, slot).start()

            base = pl.multiple_of(c * CHUNK, CHUNK)
            for m in range(mixed):
                rep[pl.ds(base, CHUNK), m * hd : (m + 1) * hd] = wide[
                    pl.ds(m, CHUNK, stride=mixed), :
                ].astype(BF16)
            return carry

        lax.fori_loop(0, chunks, body, 0)

    def send(src, dst, phase, peer):
        return pltpu.make_async_remote_copy(
            src_ref=src,
            dst_ref=dst,
            send_sem=send_sem.at[phase, peer],
            recv_sem=recv_sem.at[phase, me],
            device_id={"head": peer},
            device_id_type=MESH,
        )

    def peer_at(k):
        return lax.rem(me + k, n)

    def arrive(buf, phase, src):
        pltpu.make_async_copy(buf.at[src], buf.at[src], recv_sem.at[phase, src]).wait()

    fill(0)

    barrier = pltpu.get_barrier_semaphore()
    for k in range(1, n):
        pl.semaphore_signal(
            barrier, inc=1, device_id={"head": peer_at(k)}, device_id_type=MESH
        )
    pl.semaphore_wait(barrier, n - 1)

    def gather_start(layer, src):
        for k in range(1, n):
            send(src, xg.at[layer, me], 2 * layer, peer_at(k)).start()
        pltpu.make_async_copy(src, xg.at[layer, me], own_sem.at[0]).start()

    def gather_wait(layer, src):
        for k in range(1, n):
            arrive(xg.at[layer], 2 * layer, peer_at(k))
        pltpu.make_async_copy(src, xg.at[layer, me], own_sem.at[0]).wait()

    def project(layer):
        total = jnp.zeros((rows, 1), F32)
        for i in range(n):
            block = xg[layer, i].astype(F32)
            total = total + jnp.sum(block * block, axis=-1, keepdims=True)
            gain = gains_ref[layer, :, i * shard : (i + 1) * shard]
            lhs[:, i * shard : (i + 1) * shard] = (block * gain).astype(BF16)
        for at in range(0, mixed * hd, 2 * hd):
            stop = min(at + 2 * hd, mixed * hd)
            acc[:, at:stop] = jnp.dot(
                lhs[...], rep[:, at:stop], preferred_element_type=F32
            )
        return lax.rsqrt(total / width + EPSILON)

    def norm(v):
        return v * lax.rsqrt(jnp.mean(v * v, axis=-1, keepdims=True) + EPSILON)

    def dots(a, b):
        return jnp.sum(a * b, axis=-1, keepdims=True)

    def tok(t):
        return slice(t * batch, (t + 1) * batch)

    def per_pair(fn):
        step = 4 if batch % 4 == 0 else 1

        def body(i, carry):
            for j in range(step):
                b = i * step + j
                for h in range(heads):
                    fn(b, h)
            return carry

        lax.fori_loop(0, batch // step, body, 0)

    def mesa(layer, factor):
        copies = state_copies(layer)
        for h in range(heads):
            cols = [slice((j * heads + h) * hd, (j * heads + h + 1) * hd) for j in range(3)]
            kq[h, rows:, :] = norm(acc[:, cols[0]] * factor)
            kq[h, :rows, :] = norm(acc[:, cols[1]] * factor) * hd ** (-0.5)
            left_ref[layer, h, rows:, :] = acc[:, cols[2]] * factor
        copies[0].wait()

        def first(b, h):
            pair = kq[h, pl.ds(b, 2 * tokens, stride=batch), :].astype(BF16)
            pz[h, pl.ds(b, 2 * tokens, stride=batch), :] = jnp.dot(
                pair, rv[layer, b, h].astype(BF16), preferred_element_type=F32
            )

        per_pair(first)
        for h in range(heads):
            g = jnp.full((batch, 1), dec_ref[layer, h], F32)
            ginv = 1.0 / g
            ks = [kq[h, tok(t), :] for t in range(tokens)]
            qs = [kq[h, tok(tokens + t), :] for t in range(tokens)]
            ps = [pz[h, tok(t), :] for t in range(tokens)]
            zs = [pz[h, tok(tokens + t), :] for t in range(tokens)]
            back = [None] * (tokens + 1)
            front = [None] * (tokens + 1)
            back[0] = front[0] = jnp.ones_like(g)
            for t in range(tokens):
                back[t + 1] = back[t] * ginv
                front[t + 1] = front[t] * g
            for t in range(tokens):
                u = ps[t]
                inv = 1.0 / (g + dots(ks[t], u))
                for s in range(t + 1, tokens):
                    ps[s] = (ps[s] - u * (dots(u, ks[s]) * inv)) * ginv
                for s in range(t, tokens):
                    zs[s] = (zs[s] - u * (dots(u, qs[s]) * inv)) * ginv
                left_ref[layer, h, tok(t), :] = u
                right_ref[layer, h, tok(t), :] = u * (-inv * back[tokens - t])
                right_ref[layer, h, tok(tokens + t), :] = ks[t] * front[tokens - 1 - t]
                pz[h, tok(t), :] = zs[t]
        copies[1].wait()

        def second(b, h):
            pair = pz[h, pl.ds(b, 2 * tokens, stride=batch), :].astype(BF16)
            os[h, pl.ds(b, 2 * tokens, stride=batch), :] = lax.dot_general(
                pair, sv[layer, b, h].astype(BF16), (((1,), (1,)), ((), ())),
                preferred_element_type=F32,
            )

        per_pair(second)
        for h in range(heads):
            g = jnp.full((batch, 1), dec_ref[layer, h], F32)
            front = [jnp.ones_like(g)]
            for t in range(tokens):
                front.append(front[-1] * g)
            for t in range(tokens):
                w = pz[h, tok(t), :]
                out = os[h, tok(t), :] * front[t + 1]
                for s in range(t + 1):
                    v = left_ref[layer, h, tok(tokens + s), :]
                    out = out + v * (dots(kq[h, tok(s), :], w) * front[t - s])
                oo[tok(t), h * hd : (h + 1) * hd] = out.astype(BF16)
        copies[2].wait()

    def mix(layer):
        phase = 2 * layer + 1
        for k in list(range(1, n)):
            p = peer_at(k)
            col = pl.ds(pl.multiple_of(p * shard, shard), shard)
            part[layer, p] = jnp.dot(
                oo[...], wo[layer, :, col], preferred_element_type=F32
            ).astype(BF16)
            send(part.at[layer, p], recv.at[layer, me], phase, p).start()
        col = pl.ds(pl.multiple_of(me * shard, shard), shard)
        return jnp.dot(oo[...], wo[layer, :, col], preferred_element_type=F32)

    def collect(layer):
        total = cur[...]
        for k in range(1, n):
            p = peer_at(k)
            arrive(recv.at[layer], 2 * layer + 1, p)
            total = total + recv[layer, p].astype(F32)
        return total

    gather_start(0, x_ref)
    repack(0)
    for layer in range(layers):
        for copy in state_copies(layer):
            copy.start()
    if layers > 1:
        fill(1)
    cur[...] = x_ref[...].astype(F32)
    gather_wait(0, x_ref)
    for layer in range(layers):
        factor = project(layer)
        mesa(layer, factor)
        cur[...] = cur[...] + mix(layer)
        if layer + 1 < layers:
            repack(layer + 1)
            if layer + 2 < layers:
                fill(layer + 2)
            total = collect(layer)
            cur[...] = total
            xg[layer + 1, me] = total.astype(BF16)
            for k in range(1, n):
                send(
                    xg.at[layer + 1, me], xg.at[layer + 1, me], 2 * layer + 2, peer_at(k)
                ).start()
            for k in range(1, n):
                arrive(xg.at[layer + 1], 2 * layer + 2, peer_at(k))
        else:
            y_ref[...] = collect(layer)
    for layer in range(layers):
        for k in range(1, n):
            p = peer_at(k)
            send(x_ref, xg.at[layer, me], 2 * layer, p).wait_send()
            send(part.at[layer, p], recv.at[layer, me], 2 * layer + 1, p).wait_send()


def state_kernel(tokens, batch, heads, dec_ref, left_ref, right_ref, r_ref, s_ref, s_out, r_out):
    layer = pl.program_id(0)
    step = pl.program_id(1)
    count = r_ref.shape[1]
    hd = r_ref.shape[-1]
    upper = lax.broadcasted_iota(jnp.int32, (2 * tokens, hd), 0) < tokens
    for i in range(count):
        b = step * count + i
        for h in range(heads):
            g = jnp.full((1, hd), dec_ref[layer, h], F32)
            power = g
            for _ in range(tokens - 1):
                power = power * g
            rows = pl.ds(b, 2 * tokens, stride=batch)
            left = left_ref[0, h, rows, :]
            right = right_ref[0, h, rows, :]
            zero = jnp.zeros_like(right)
            both = jnp.concatenate(
                [jnp.where(upper, right, zero), jnp.where(upper, zero, right)], axis=1
            ).astype(BF16)
            update = jnp.dot(left.T.astype(BF16), both, preferred_element_type=F32)
            r_out[0, i, h] = r_ref[0, i, h] * (1.0 / power) + update[:, :hd]
            s_out[0, i, h] = s_ref[0, i, h] * power + update[:, hd:]


def on_device(n, inputs, gains, decays, w_qkv, w_out, s_state, r_state):
    layers, width, _, heads, hd = w_qkv.shape
    tokens, batch, shard = inputs.shape
    rows = tokens * batch
    mixed = 3 * heads
    vmem = pl.BlockSpec(memory_space=pltpu.VMEM)
    smem = pl.BlockSpec(memory_space=pltpu.SMEM)
    anywhere = pl.BlockSpec(memory_space=pl.ANY)
    pairs = (layers, heads, 2 * rows, hd)
    y, left, right = pl.pallas_call(
        functools.partial(front_kernel, n, tokens, batch, heads, layers),
        out_shape=(
            jax.ShapeDtypeStruct((rows, shard), F32),
            jax.ShapeDtypeStruct(pairs, F32),
            jax.ShapeDtypeStruct(pairs, F32),
        ),
        in_specs=[vmem, vmem, smem, anywhere, anywhere, anywhere, anywhere],
        out_specs=(vmem, vmem, vmem),
        scratch_shapes=[
            pltpu.VMEM((RING, CHUNK * mixed, hd), BF16),
            pltpu.VMEM((CHUNK * mixed, hd), F32),
            pltpu.VMEM((width, mixed * hd), BF16),
            pltpu.VMEM((layers, heads * hd, width), BF16),
            pltpu.VMEM((layers, batch, heads, hd, hd), F32),
            pltpu.VMEM((layers, batch, heads, hd, hd), F32),
            pltpu.VMEM((layers, n, rows, shard), BF16),
            pltpu.VMEM((rows, width), BF16),
            pltpu.VMEM((rows, mixed * hd), F32),
            pltpu.VMEM((layers, n, rows, shard), BF16),
            pltpu.VMEM((layers, n, rows, shard), BF16),
            pltpu.VMEM((rows, shard), F32),
            pltpu.VMEM((heads, 2 * rows, hd), F32),
            pltpu.VMEM((heads, 2 * rows, hd), F32),
            pltpu.VMEM((heads, 2 * rows, hd), F32),
            pltpu.VMEM((rows, heads * hd), BF16),
            pltpu.SemaphoreType.DMA((RING,)),
            pltpu.SemaphoreType.DMA((3, layers)),
            pltpu.SemaphoreType.DMA((2 * layers, n)),
            pltpu.SemaphoreType.DMA((2 * layers, n)),
            pltpu.SemaphoreType.DMA((1,)),
        ],
        compiler_params=pltpu.CompilerParams(
            collective_id=0, has_side_effects=True, vmem_limit_bytes=62 * 1024 * 1024
        ),
        name="front",
    )(
        inputs.reshape(rows, shard),
        gains.reshape(layers, 1, width),
        decays,
        w_qkv.reshape(layers, width * mixed, hd),
        w_out.reshape(layers, heads * hd, width),
        s_state,
        r_state,
    )
    count = 4 if batch % 4 == 0 else 1
    block = pl.BlockSpec((1, count, heads, hd, hd), lambda l, b: (l, b, 0, 0, 0))
    side = pl.BlockSpec((1, heads, 2 * rows, hd), lambda l, b: (l, 0, 0, 0))
    s_final, r_final = pl.pallas_call(
        functools.partial(state_kernel, tokens, batch, heads),
        grid=(layers, batch // count),
        out_shape=(
            jax.ShapeDtypeStruct(s_state.shape, F32),
            jax.ShapeDtypeStruct(r_state.shape, F32),
        ),
        in_specs=[smem, side, side, block, block],
        out_specs=(block, block),
        compiler_params=pltpu.CompilerParams(
            dimension_semantics=("arbitrary", "arbitrary")
        ),
        name="states",
    )(decays, left, right, r_state, s_state)
    return y.reshape(tokens, batch, shard), s_final, r_final


def solution(mesh):
    in_specs = (
        P(None, "grp", "head"),
        P(),
        P(None, "head"),
        P(None, None, None, "head", None),
        P(None, "head", None, None),
        P(None, "grp", "head", None, None),
        P(None, "grp", "head", None, None),
    )
    out_specs = (
        P(None, "grp", "head"),
        P(None, "grp", "head", None, None),
        P(None, "grp", "head", None, None),
    )
    return jax.shard_map(
        functools.partial(on_device, mesh.shape["head"]),
        mesh=mesh,
        in_specs=in_specs,
        out_specs=out_specs,
        check_vma=False,
    )
```

profile of v0, /device:TPU:1, one launch (start us, length us, event | category | flops | bytes accessed | tf_op | source)
XLA Modules:
  0.0 65.4 jit_solution(7386918571674972795)
XLA Ops:
  0.6 1.4 %reshape.22.gains_ref = f32[2,1,4096]{2,1,0:T(1,128)} reshape(f32[2,4096]{1,0:T(2,128)} %param.8) | data formatting | bytes 65536 | tf_op jit(solution)/shard_map/reshape | solution.py:332
  2.0 47.4 %front.1 = (f32[64,512]{1,0:T(8,128)}, f32[2,4,128,128]{3,2,1,0:T(8,128)}, f32[2,4,128,128]{3,2,1,0:T(8,128)}) custom-call(bf16[64,512]{1,0:T(8,128)(2,1)} %bitcast.7, f32[2,1,4096]{2,1,0:T(1,128)} %reshape.22.gains_ref, f32[2,4]{1,0:T(2,128)} %dec_ref.3, bf16[2,49152,128]{2,1,0:T(8,128)(2,1)} %bitcast.4, bf16[2,512,4096]{2,1,0:T(8,128)(2,1)} %bitcast.5, ...), custom_call_target="tpu_custom_call" | custom-call | tf_op jit(solution)/shard_map/front/pallas_call | solution.py:294
  49.5 0.0 copy-start
  49.5 15.2 %states.1 = (f32[2,16,4,128,128]{4,3,2,1,0:T(8,128)}, f32[2,16,4,128,128]{4,3,2,1,0:T(8,128)}) custom-call(f32[2,4]{1,0:T(2,128)} %dec_ref.3, f32[2,4,128,128]{3,2,1,0:T(8,128)} %get-tuple-element.9.left_ref, f32[2,4,128,128]{3,2,1,0:T(8,128)} %get-tuple-element.10.right_ref, f32[2,16,4,128,128]{4,3,2,1,0:T(8,128)} %r_ref.1, f32[2,16,4,128,128]{4,3,2,1,0:T(8,128)} %s_ref.1), custom_call_target="tpu_custom_call" | custom-call | tf_op jit(solution)/shard_map/states/pallas_call | solution.py:342
  64.7 0.0 copy-done
  64.7 0.7 %copy.11 = f32[4,16,512]{2,1,0:T(8,128)} copy(f32[4,16,512]{2,1,0:T(8,128)S(1)} %bitcast.6) | data formatting | bytes 262144
Async XLA Ops:
  49.5 15.2 %copy-start = (f32[64,512]{1,0:T(8,128)S(1)}, f32[64,512]{1,0:T(8,128)}, u32[]{:S(2)}) copy-start(f32[64,512]{1,0:T(8,128)} %get-tuple-element.8) | copy-start | bytes 393220
where the time goes:
time: 65.8 us; the launch traced here: 65.4 us
  Pallas kernels  62.7 us (95%)
  local copies, waits for them, and re-layouts  2.06 us (3%)
    pallas_call x1, Pallas kernels, on_device(): pl.pallas_call(functools.partial(front_kernel, n, tokens, batch, heads, l...  47.4 us
    pallas_call x1, Pallas kernels, on_device(): pl.pallas_call(functools.partial(state_kernel, tokens, batch, heads), gri...  15.2 us
    reshape x1, local copies, waits for them, and re-layouts, on_device(): gains.reshape(layers, 1, width)  1.4 us

commit v1 on v0

--- a/solution.py
+++ b/solution.py
@@ -18,8 +18,8 @@
 def front_kernel(
     n, tokens, batch, heads, layers,
     x_ref, gains_ref, dec_ref, w_hbm, wo_hbm, s_hbm, r_hbm,
-    y_ref, left_ref, right_ref,
-    raw, wide, rep, wo, sv, rv, xg, lhs, acc, part, recv, cur, kq, pz, os, oo,
+    y_ref, sv, rv,
+    left_ref, right_ref, raw, wide, rep, wo, xg, lhs, acc, part, recv, cur, kq, pz, os, oo,
     raw_sem, in_sem, send_sem, recv_sem, own_sem,
 ):
     me = lax.axis_index("head")
@@ -202,6 +202,30 @@
                 oo[tok(t), h * hd : (h + 1) * hd] = out.astype(BF16)
         copies[2].wait()
 
+    def update(layer):
+        upper = lax.broadcasted_iota(jnp.int32, (2 * tokens, hd), 0) < tokens
+        scales = []
+        for h in range(heads):
+            g = jnp.full((1, hd), dec_ref[layer, h], F32)
+            power = g
+            for _ in range(tokens - 1):
+                power = power * g
+            scales.append((power, 1.0 / power))
+
+        def pair(b, h):
+            near = pl.ds(b, 2 * tokens, stride=batch)
+            left = left_ref[layer, h, near, :]
+            right = right_ref[layer, h, near, :]
+            zero = jnp.zeros_like(right)
+            both = jnp.concatenate(
+                [jnp.where(upper, right, zero), jnp.where(upper, zero, right)], axis=1
+            ).astype(BF16)
+            change = jnp.dot(left.T.astype(BF16), both, preferred_element_type=F32)
+            rv[layer, b, h] = rv[layer, b, h] * scales[h][1] + change[:, :hd]
+            sv[layer, b, h] = sv[layer, b, h] * scales[h][0] + change[:, hd:]
+
+        per_pair(pair)
+
     def mix(layer):
         phase = 2 * layer + 1
         for k in list(range(1, n)):
@@ -246,40 +270,17 @@
                 send(
                     xg.at[layer + 1, me], xg.at[layer + 1, me], 2 * layer + 2, peer_at(k)
                 ).start()
+            update(layer)
             for k in range(1, n):
                 arrive(xg.at[layer + 1], 2 * layer + 2, peer_at(k))
         else:
+            update(layer)
             y_ref[...] = collect(layer)
     for layer in range(layers):
         for k in range(1, n):
             p = peer_at(k)
             send(x_ref, xg.at[layer, me], 2 * layer, p).wait_send()
             send(part.at[layer, p], recv.at[layer, me], 2 * layer + 1, p).wait_send()
-
-
-def state_kernel(tokens, batch, heads, dec_ref, left_ref, right_ref, r_ref, s_ref, s_out, r_out):
-    layer = pl.program_id(0)
-    step = pl.program_id(1)
-    count = r_ref.shape[1]
-    hd = r_ref.shape[-1]
-    upper = lax.broadcasted_iota(jnp.int32, (2 * tokens, hd), 0) < tokens
-    for i in range(count):
-        b = step * count + i
-        for h in range(heads):
-            g = jnp.full((1, hd), dec_ref[layer, h], F32)
-            power = g
-            for _ in range(tokens - 1):
-                power = power * g
-            rows = pl.ds(b, 2 * tokens, stride=batch)
-            left = left_ref[0, h, rows, :]
-            right = right_ref[0, h, rows, :]
-            zero = jnp.zeros_like(right)
-            both = jnp.concatenate(
-                [jnp.where(upper, right, zero), jnp.where(upper, zero, right)], axis=1
-            ).astype(BF16)
-            update = jnp.dot(left.T.astype(BF16), both, preferred_element_type=F32)
-            r_out[0, i, h] = r_ref[0, i, h] * (1.0 / power) + update[:, :hd]
-            s_out[0, i, h] = s_ref[0, i, h] * power + update[:, hd:]
 
 
 def on_device(n, inputs, gains, decays, w_qkv, w_out, s_state, r_state):
@@ -291,22 +292,22 @@
     smem = pl.BlockSpec(memory_space=pltpu.SMEM)
     anywhere = pl.BlockSpec(memory_space=pl.ANY)
     pairs = (layers, heads, 2 * rows, hd)
-    y, left, right = pl.pallas_call(
+    y, s_new, r_new = pl.pallas_call(
         functools.partial(front_kernel, n, tokens, batch, heads, layers),
         out_shape=(
-            jax.ShapeDtypeStruct((rows, shard), F32),
-            jax.ShapeDtypeStruct(pairs, F32),
-            jax.ShapeDtypeStruct(pairs, F32),
+            pltpu.VMEM((rows, shard), F32),
+            pltpu.VMEM(s_state.shape, F32),
+            pltpu.VMEM(r_state.shape, F32),
         ),
         in_specs=[vmem, vmem, smem, anywhere, anywhere, anywhere, anywhere],
         out_specs=(vmem, vmem, vmem),
         scratch_shapes=[
+            pltpu.VMEM(pairs, F32),
+            pltpu.VMEM(pairs, F32),
             pltpu.VMEM((RING, CHUNK * mixed, hd), BF16),
             pltpu.VMEM((CHUNK * mixed, hd), F32),
             pltpu.VMEM((width, mixed * hd), BF16),
             pltpu.VMEM((layers, heads * hd, width), BF16),
-            pltpu.VMEM((layers, batch, heads, hd, hd), F32),
-            pltpu.VMEM((layers, batch, heads, hd, hd), F32),
             pltpu.VMEM((layers, n, rows, shard), BF16),
             pltpu.VMEM((rows, width), BF16),
             pltpu.VMEM((rows, mixed * hd), F32),
@@ -324,7 +325,7 @@
             pltpu.SemaphoreType.DMA((1,)),
         ],
         compiler_params=pltpu.CompilerParams(
-            collective_id=0, has_side_effects=True, vmem_limit_bytes=62 * 1024 * 1024
+            collective_id=0, has_side_effects=True, vmem_limit_bytes=42 * 1024 * 1024
         ),
         name="front",
     )(
@@ -336,24 +337,7 @@
         s_state,
         r_state,
     )
-    count = 4 if batch % 4 == 0 else 1
-    block = pl.BlockSpec((1, count, heads, hd, hd), lambda l, b: (l, b, 0, 0, 0))
-    side = pl.BlockSpec((1, heads, 2 * rows, hd), lambda l, b: (l, 0, 0, 0))
-    s_final, r_final = pl.pallas_call(
-        functools.partial(state_kernel, tokens, batch, heads),
-        grid=(layers, batch // count),
-        out_shape=(
-            jax.ShapeDtypeStruct(s_state.shape, F32),
-            jax.ShapeDtypeStruct(r_state.shape, F32),
-        ),
-        in_specs=[smem, side, side, block, block],
-        out_specs=(block, block),
-        compiler_params=pltpu.CompilerParams(
-            dimension_semantics=("arbitrary", "arbitrary")
-        ),
-        name="states",
-    )(decays, left, right, r_state, s_state)
-    return y.reshape(tokens, batch, shard), s_final, r_final
+    return y.reshape(tokens, batch, shard), s_new, r_new
 
 
 def solution(mesh):

time: 65.8 us -> 56.2 us (0.85)
  Pallas kernels: 62.7 us -> 46.4 us
  local copies, waits for them, and re-layouts: 2.06 us -> 8.85 us
    pallas_call x1 -> x0, Pallas kernels: 15.2 us -> none  [on_device(): pl.pallas_call(functools.partial(state_kernel, tokens, batch, heads), gri...]
    unnamed x3, local copies, waits for them, and re-layouts: 0.66 us -> 7.45 us
    pallas_call x1, Pallas kernels: 47.4 us -> 46.4 us  [on_device(): pl.pallas_call(functools.partial(front_kernel, n, tokens, batch, heads, l...]
where the time goes in v1:
time: 56.2 us; the launch traced here: 55.9 us
  Pallas kernels  46.4 us (83%)
  local copies, waits for them, and re-layouts  8.85 us (16%)
  between operations  0.64 us (1%)
    pallas_call x1, Pallas kernels, on_device(): pl.pallas_call(functools.partial(front_kernel, n, tokens, batch, heads, l...  46.4 us
    unnamed x3, local copies, waits for them, and re-layouts  7.45 us
    reshape x1, local copies, waits for them, and re-layouts, on_device(): gains.reshape(layers, 1, width)  1.4 us

profile of v1, /device:TPU:1, one launch (start us, length us, event | category | flops | bytes accessed | tf_op | source)
XLA Modules:
  0.0 55.9 jit_solution(7271887168276777368)
XLA Ops:
  0.6 1.4 %reshape.22.gains_ref = f32[2,1,4096]{2,1,0:T(1,128)} reshape(f32[2,4096]{1,0:T(2,128)} %param.8) | data formatting | bytes 65536 | tf_op jit(solution)/shard_map/reshape | solution.py:333
  2.0 46.4 %front.1 = (f32[64,512]{1,0:T(8,128)S(1)}, f32[2,16,4,128,128]{4,3,2,1,0:T(8,128)S(1)}, f32[2,16,4,128,128]{4,3,2,1,0:T(8,128)S(1)}) custom-call(bf16[64,512]{1,0:T(8,128)(2,1)} %bitcast.7, f32[2,1,4096]{2,1,0:T(1,128)} %reshape.22.gains_ref, f32[2,4]{1,0:T(2,128)} %dec_ref.1, bf16[2,49152,128]{2,1,0:T(8,128)(2,1)} %bitcast.5, ...), custom_call_target="tpu_custom_call" | custom-call | tf_op jit(solution)/shard_map/front/pallas_call | solution.py:295
  48.5 0.7 %copy.13 = f32[4,16,512]{2,1,0:T(8,128)} copy(f32[4,16,512]{2,1,0:T(8,128)S(1)} %bitcast.4) | data formatting | bytes 262144
  49.1 3.4 %copy.14 = f32[2,16,4,128,128]{4,3,2,1,0:T(8,128)} copy(f32[2,16,4,128,128]{4,3,2,1,0:T(8,128)S(1)} %get-tuple-element.10) | data formatting | bytes 16777216
  52.5 3.4 %copy.15 = f32[2,16,4,128,128]{4,3,2,1,0:T(8,128)} copy(f32[2,16,4,128,128]{4,3,2,1,0:T(8,128)S(1)} %get-tuple-element.11) | data formatting | bytes 16777216
